TPU v7x, 32 devices: a whole 2x2x4 slice. The times are simulated.
32 devices in a mesh: dp: 8 (over y, x, core), tensor: 4 (over z).
Axes of the slice: x: 2, y: 2, z: 4, core: 2. Of those that a mesh axis runs over, the one named last changes fastest.
Arguments:
- inputs: bfloat16 [16384, 768], P('dp'), may hold values from -6 to 6
- cotangent: bfloat16 [16384, 768], P('dp'), may hold values from -6 to 6
- counts: int32 [32], P('dp'), may hold values from 40 to 512, as said below
- keep_mask: int32 [16384], P('dp'), may hold values 0 or 1
- box_x: int32 [16384], P('dp'), may hold values from 0 to 63
- box_y: int32 [16384], P('dp'), may hold values from 0 to 63
- gain_one: float32 [768], replicated, may hold values from 0.5 to 1.5
- shift_one: float32 [768], replicated, may hold values from -4 to 4
- w_qkv: bfloat16 [3, 768, 768], P(None, None, 'tensor'), may hold values from -0.21875 to 0.21875
- b_qv: float32 [2, 768], P(None, 'tensor'), may hold values from -4 to 4
- w_out: bfloat16 [768, 768], P('tensor'), may hold values from -0.875 to 0.875
- b_out: float32 [768], replicated, may hold values from -4 to 4
- gain_two: float32 [768], replicated, may hold values from 0.5 to 1.5
- shift_two: float32 [768], replicated, may hold values from -4 to 4
- w_up: bfloat16 [768, 3072], P(None, 'tensor'), may hold values from -0.21875 to 0.21875
- b_up: float32 [3072], P('tensor'), may hold values from -4 to 4
- w_down: bfloat16 [3072, 768], P('tensor'), may hold values from -0.109375 to 0.109375
- b_down: float32 [768], replicated, may hold values from -4 to 4
- rel_tables: float32 [2, 12, 64], P(None, 'tensor'), may hold values from -4 to 4
Outputs:
- out: bfloat16 [16384, 768], P('dp')
- grad_input: bfloat16 [16384, 768], P('dp')
- grad_w_qkv: float32 [3, 768, 768], P(None, None, 'tensor')
- grad_b_qv: float32 [2, 768], P(None, 'tensor')
- grad_w_out: float32 [768, 768], P('tensor')
- grad_b_out: float32 [768], replicated
- grad_gain_one: float32 [768], replicated
- grad_shift_one: float32 [768], replicated
- grad_gain_two: float32 [768], replicated
- grad_shift_two: float32 [768], replicated
- grad_w_up: float32 [768, 3072], P(None, 'tensor')
- grad_b_up: float32 [3072], P('tensor')
- grad_w_down: float32 [3072, 768], P('tensor')
- grad_b_down: float32 [768], replicated
- grad_tables: float32 [2, 12, 64], P(None, 'tensor')
Inputs may be any that keep to these rules, and one draw needn't show every extreme that they name: The first counts[p] slots of page p hold tokens and the rest are padding; in every draw some page has all 512 slots in use.
All inputs are finite; a program needn't handle non-finite values. No bound on the sum of `keep_mask` on one device may be relied on, other than what follows from the above.
Results may differ from a plain program's by a relative error of at most 0.017.
Values may be sent and summed in bfloat16 or wider, within the bound.
A program may use at most 128 MiB of HBM per device.

v0:
```python
import functools
import jax
import jax.numpy as jnp
from jax import lax
from jax.experimental import pallas as pl
from jax.experimental.pallas import tpu as pltpu
from jax.sharding import PartitionSpec as P

HEAD_DIM = 64
PAGE = 512
BLOCK = 128
epsilon = 1e-05
masked_score = -1e30
LOG2E = 1.4426950408889634
LN2 = 0.6931471805599453
bf16 = jnp.bfloat16
f32 = jnp.float32
VMEM_LIMIT = 60 << 20


def dot(left, right, left_dim, right_dim):
    return lax.dot_general(
        left, right, (((left_dim,), (right_dim,)), ((), ())), preferred_element_type=f32
    )


def nn(left, right):
    return dot(left, right, 1, 0)


def nt(left, right):
    return dot(left, right, 1, 1)


def tn(left, right):
    return dot(left, right, 0, 0)


def norm_parts(rows):
    average = jnp.mean(rows, axis=-1, keepdims=True)
    centered = rows - average
    variance = jnp.mean(centered * centered, axis=-1, keepdims=True)
    inverse = lax.rsqrt(variance + epsilon)
    return centered * inverse, inverse


def norm_grad(grad_out, xhat, inverse, gain):
    scaled = grad_out * gain
    mean_one = jnp.mean(scaled, axis=-1, keepdims=True)
    mean_two = jnp.mean(scaled * xhat, axis=-1, keepdims=True)
    return inverse * (scaled - mean_one - xhat * mean_two)


def one_hot_columns(box_x_ref, box_y_ref, bins, reverse=False):
    width = box_x_ref.shape[-1]
    levels = lax.broadcasted_iota(jnp.int32, (bins, width), 0)
    if reverse:
        levels = (bins - 1) - levels
    hot_x = jnp.where(levels == box_x_ref[0], 1.0, 0.0)
    hot_y = jnp.where(levels == box_y_ref[0], 1.0, 0.0)
    return jnp.concatenate([hot_x, hot_y], axis=0).astype(bf16)


def by_halves(count, body):
    body(PAGE)


def neighbours(axis):
    core = axis % 2
    side_x = (axis // 2) % 2
    side_y = (axis // 4) % 2
    return core, side_x, side_y, 1 - 2 * core, 2 - 4 * side_x, 4 - 8 * side_y


def flipped(index, mask):
    result, bit = index, 1
    while bit <= mask:
        if mask & bit:
            result = result + bit - 2 * bit * ((index // bit) % 2)
        bit *= 2
    return result


def greet(peers):
    barrier = pltpu.get_barrier_semaphore()
    for dp, tensor in peers:
        pl.semaphore_signal(
            barrier, inc=1, device_id={"dp": dp, "tensor": tensor}, device_id_type=pl.DeviceIdType.MESH
        )
    pl.semaphore_wait(barrier, len(peers))


KIND_Z, KIND_X, KIND_Y, KIND_VIA_X, KIND_VIA_Y, KIND_CORE = 0, 1, 2, 3, 4, 5
KINDS = 9


def gather_steps(shards, sources, targets, small_sources, small_targets, send_sem, recv_sem):
    arrays = len(sources)
    place = lax.axis_index("tensor")
    lane = lax.axis_index("dp")
    core, side_x, side_y, to_core, to_x, to_y = neighbours(lane)
    mine = lane % 8
    rows = targets[0].shape[1] // 8
    half = rows // 2
    hops = range(1, shards)

    def piece(index, start=0, size=rows):
        return pl.ds(pl.multiple_of(index * rows + start, 16), size)

    def remote(kind, array, hop, source, target, dp, tensor):
        return pltpu.make_async_remote_copy(
            src_ref=source,
            dst_ref=target,
            send_sem=send_sem.at[kind, array, hop - 1],
            recv_sem=recv_sem.at[kind, array, hop - 1],
            device_id={"dp": dp, "tensor": tensor},
            device_id_type=pl.DeviceIdType.MESH,
        )

    def within(kind, array, hop, region, step):
        ref = targets[array].at[flipped(place, hop), region]
        return remote(kind, array, hop, ref, ref, lane + step, place)

    def along(array, hop):
        source, target = sources[array].at[piece(mine)], targets[array].at[place, piece(mine)]
        return remote(KIND_Z, array, hop, source, target, lane, flipped(place, hop))

    def along_small(index, hop):
        source, target = small_sources[index], small_targets[index].at[place]
        return remote(1 + index, arrays, hop, source, target, lane, flipped(place, hop))

    def enter():
        greet(
            [(lane + step, place) for step in (to_core, to_x, to_y)] + [(lane, flipped(place, hop)) for hop in hops]
        )

    def begin():
        for array in range(arrays):
            for hop in hops:
                along(array, hop).start()
            if array == 0:
                for index in range(len(small_sources)):
                    for hop in hops:
                        along_small(index, hop).start()

    def arrive(array, hop):
        along(array, hop).wait_recv()
        within(KIND_X, array, hop, piece(mine), to_x).start()
        within(KIND_Y, array, hop, piece(mine), to_y).start()
        within(KIND_CORE, array, hop, piece(mine), to_core).start()

    def spread_near(array, hop):
        at = mine + to_x
        within(KIND_X, array, hop, piece(at), to_x).wait_recv()
        within(KIND_VIA_Y, array, hop, piece(at, 0, half), to_y).start()
        within(KIND_CORE + 1, array, hop, piece(at), to_core).start()
        at = mine + to_y
        within(KIND_Y, array, hop, piece(at), to_y).wait_recv()
        within(KIND_VIA_X, array, hop, piece(at, half, half), to_x).start()
        within(KIND_CORE + 2, array, hop, piece(at), to_core).start()

    def spread_far(array, hop):
        at = mine + to_x + to_y
        within(KIND_VIA_Y, array, hop, piece(at, 0, half), to_y).wait_recv()
        within(KIND_VIA_X, array, hop, piece(at, half, half), to_x).wait_recv()
        within(KIND_CORE + 3, array, hop, piece(at), to_core).start()

    def finish(array, hop):
        for index, shift in enumerate((0, to_x, to_y, to_x + to_y)):
            within(KIND_CORE + index, array, hop, piece(mine + to_core + shift), to_core).wait_recv()

    def drain(early):
        for hop in hops:
            if early:
                for index in range(len(small_sources)):
                    along_small(index, hop).wait()
                continue
            for array in range(arrays):
                along(array, hop).wait_send()
                within(KIND_X, array, hop, piece(mine), to_x).wait_send()
                within(KIND_Y, array, hop, piece(mine), to_y).wait_send()
                within(KIND_VIA_Y, array, hop, piece(mine + to_x, 0, half), to_y).wait_send()
                within(KIND_VIA_X, array, hop, piece(mine + to_y, half, half), to_x).wait_send()
                for index, shift in enumerate((0, to_x, to_y, to_x + to_y)):
                    within(KIND_CORE + index, array, hop, piece(mine + shift), to_core).wait_send()

    items = [(array, hop) for array in range(arrays) for hop in hops]
    stages = (arrive, spread_near, spread_far, finish)

    def tick(at):
        for stage, act in enumerate(stages):
            if 0 <= at - stage < len(items):
                act(*items[at - stage])

    return enter, begin, tick, len(items) + len(stages) - 1, drain


def gather_semaphores(arrays, shards):
    return [pltpu.SemaphoreType.DMA((KINDS, arrays + 1, shards - 1))] * 2


def forward_kernel(
    shards,
    counts_ref,
    x_ref,
    keep_ref,
    box_x_ref,
    box_y_ref,
    rows_ref,
    bias_ref,
    tables_ref,
    qkv_weight_ref,
    out_weight_ref,
    up_ref,
    down_ref,
    qkv_ref,
    probs_ref,
    inverse_ref,
    context_ref,
    hidden_ref,
    gathered_ref,
    up_all_ref,
    down_all_ref,
    rows_all_ref,
    weights,
    copy_sem,
    bounce,
    bias_all,
    tables_all,
    send_sem,
    recv_sem,
    bias_columns,
    toeplitz,
    spread,
    scores,
):
    page = pl.program_id(0)
    pages = counts_ref.shape[0]
    place = lax.axis_index("tensor")
    width, model = x_ref.shape
    heads = model // HEAD_DIM
    own = model // shards
    own_heads = heads // shards
    bins = tables_ref.shape[-1]
    split = qkv_weight_ref.shape[0]
    smalls, small_targets = (rows_ref, bias_ref, tables_ref), (rows_all_ref, bias_all, tables_all)
    enter, begin, tick, ticks, drain = gather_steps(
        shards,
        (bounce.at[0], up_ref, down_ref),
        (gathered_ref, up_all_ref, down_all_ref),
        smalls,
        small_targets,
        send_sem,
        recv_sem,
    )
    loads = [
        pltpu.make_async_copy(qkv_weight_ref, bounce.at[0, 0:split], copy_sem.at[0]),
        pltpu.make_async_copy(out_weight_ref, bounce.at[0, split:], copy_sem.at[1]),
        pltpu.make_async_copy(up_ref, bounce.at[1], copy_sem.at[2]),
        pltpu.make_async_copy(down_ref, bounce.at[2], copy_sem.at[3]),
    ]
    stores = [
        pltpu.make_async_copy(bounce.at[index], target.at[place], copy_sem.at[4 + index])
        for index, target in enumerate((gathered_ref, up_all_ref, down_all_ref))
    ] + [
        pltpu.make_async_copy(source, target.at[place], copy_sem.at[7 + index])
        for index, (source, target) in enumerate(zip(smalls, small_targets))
    ]
    weight_copies = [
        pltpu.make_async_copy(
            gathered_ref.at[:, pl.ds(kind * own, own)], weights.at[kind], copy_sem.at[10 + kind]
        )
        for kind in range(4)
    ]
    before = shards - 1 + 3

    @pl.when(page == 0)
    def _():
        for copy in loads:
            copy.start()
        enter()
        for copy in loads[0:2]:
            copy.wait()
        begin()
        for copy in loads[2:4]:
            copy.wait()
        for copy in stores:
            copy.start()
        for copy in stores:
            copy.wait()
        for at in range(before):
            tick(at)
        for copy in weight_copies:
            copy.start()
        drain(True)
        for shard in range(shards):
            rows = slice(shard * own, (shard + 1) * own)
            for kind in range(2):
                wide = jnp.broadcast_to(bias_all[shard, kind : kind + 1, :], (128, own))
                bias_columns[kind, rows, :] = wide.T
        m = lax.broadcasted_iota(jnp.int32, (bins, 2 * bins), 1)
        signed = jnp.where(m >= bins, 2 * bins - m, -m)
        level = lax.broadcasted_iota(jnp.int32, (bins, 2 * bins), 0)
        pick = jnp.where(jnp.clip(signed, -(bins // 2), bins // 2 - 1) + bins // 2 == level, 1.0, 0.0).astype(bf16)
        lane = lax.broadcasted_iota(jnp.int32, (bins, 2 * bins), 1)
        for shard in range(shards):
            for one in range(own_heads):
                at = (shard * own_heads + one) * 2 * bins
                for kind in range(2):
                    table = (tables_all[shard, one, kind : kind + 1, :] * LOG2E).astype(bf16)
                    line = nn(jnp.broadcast_to(table, (bins, bins)), pick)
                    rolled = pltpu.roll(line, kind * bins, 1, stride=1, stride_axis=0)
                    inside = lane >= bins if kind else lane < bins
                    toeplitz[at + kind * bins : at + (kind + 1) * bins, :] = jnp.where(inside, rolled, 0.0).astype(bf16)
        for copy in weight_copies:
            copy.wait()

    points = 5
    left = ticks - before

    def point(index):
        for at in range(before, ticks):
            where = (at - before + 1) * points * pages // (left + 1) - 1
            if where % points == index:
                pl.when(page == where // points)(functools.partial(tick, at))

    tokens = x_ref[...].astype(f32)
    xhat, _ = norm_parts(tokens)
    low = (xhat * rows_ref[0:1, :] + rows_ref[1:2, :]).astype(bf16)
    for kind in range(3):
        product = nt(weights[kind].reshape(model, model), low)
        if kind == 0:
            product = (product + bias_columns[0, :, 0:1]) * (LOG2E * HEAD_DIM**-0.5)
        if kind == 2:
            product = product + bias_columns[1, :, 0:1]
        qkv_ref[0, kind] = product.astype(bf16)
    hot = one_hot_columns(box_x_ref, box_y_ref, bins)
    spread[...] = nn(toeplitz[...], hot).astype(bf16)
    lane = lax.broadcasted_iota(jnp.int32, (1, width), 1)
    open_key = (lane < counts_ref[page]) & (keep_ref[0] == 1)
    mask_row = jnp.where(open_key, 0.0, masked_score)
    first = lax.broadcasted_iota(jnp.int32, (HEAD_DIM, width), 0) == 0
    key_pad = jnp.where(first, mask_row, 0.0).astype(bf16)
    query_pad = jnp.where(first, 1.0, 0.0).astype(bf16)
    ones = jnp.ones((16, width), bf16)
    eye = lax.broadcasted_iota(jnp.int32, (BLOCK, BLOCK), 0) == lax.broadcasted_iota(jnp.int32, (BLOCK, BLOCK), 1)

    def score(index, slot):
        rows = slice(index * HEAD_DIM, (index + 1) * HEAD_DIM)
        query = qkv_ref[0, 0, rows]
        key = qkv_ref[0, 1, rows]
        bias = spread[index * 2 * bins : (index + 1) * 2 * bins, :]
        left = jnp.concatenate([key, key_pad, hot], axis=0)
        right = jnp.concatenate([query, query_pad, bias], axis=0)
        scores[slot] = tn(left, right)
        return jnp.sum(query.astype(f32) * key.astype(f32), axis=0, keepdims=True) + jnp.sum(
            bias.astype(f32) * hot.astype(f32), axis=0, keepdims=True
        )

    def soften(index, slot, own_score):
        for at in range(width // BLOCK):
            span = slice(at * BLOCK, (at + 1) * BLOCK)
            scores[slot, span, span] = jnp.where(eye, own_score[:, span], scores[slot, span, span])
        top = jnp.max(scores[slot], axis=0, keepdims=True)
        probs_ref[0, index] = jnp.exp2(scores[slot] - top).astype(bf16)

    def mix(index):
        rows = slice(index * HEAD_DIM, (index + 1) * HEAD_DIM)
        mixed = nn(jnp.concatenate([qkv_ref[0, 2, rows], ones], axis=0), probs_ref[0, index])
        inverse = 1.0 / mixed[HEAD_DIM : HEAD_DIM + 1]
        inverse_ref[0, index] = inverse
        context_ref[0, rows] = (mixed[0:HEAD_DIM] * inverse).astype(bf16)

    point(0)
    owns = [score(0, 0)]
    for at in range(heads):
        if at + 1 < heads:
            owns.append(score(at + 1, (at + 1) % 2))
        soften(at, at % 2, owns[at])
        if at > 0:
            mix(at - 1)
        if at % 3 == 2 and at + 1 < heads:
            point(1 + at // 3)
    mix(heads - 1)
    point(4)
    attended = tn(context_ref[0], weights[3].reshape(model, model))
    hidden_ref[...] = tokens + attended + rows_ref[2:3, :]

    @pl.when(page == pages - 1)
    def _():
        drain(False)


def mlp_kernel(
    counts_ref,
    place_ref,
    hidden_ref,
    cotangent_ref,
    rows_ref,
    bias_ref,
    up_ref,
    down_ref,
    out_ref,
    grad_hidden_ref,
    grad_up_ref,
    grad_down_ref,
    sums_ref,
    up_total,
    down_total,
    low_ref,
    gl_ref,
    down_acc,
    gn_acc,
    act_ref,
    gu_ref,
    upper_ref,
    grad_ref,
):
    page = pl.program_id(0)
    shards = up_ref.shape[0]
    place = place_ref[0]

    @pl.when(page == 0)
    def _():
        up_total[...] = jnp.zeros_like(up_total)
        down_total[...] = jnp.zeros_like(down_total)
        sums_ref[...] = jnp.zeros_like(sums_ref)

    count = counts_ref[page]

    def body(width):
        valid = lax.broadcasted_iota(jnp.int32, (width, 1), 0) < count
        hidden = hidden_ref[0:width, :]
        xhat, inverse = norm_parts(hidden)
        low = (xhat * rows_ref[3:4, :] + rows_ref[4:5, :]).astype(bf16)
        grad_result = jnp.where(valid, cotangent_ref[0:width, :].astype(f32), 0.0)
        grad_low = grad_result.astype(bf16)

        low_ref[0:width, :] = low
        gl_ref[0:width, :] = grad_low
        down_acc[0:width, :] = jnp.zeros((width, hidden.shape[1]), f32)
        gn_acc[0:width, :] = jnp.zeros((width, hidden.shape[1]), f32)

        def lead(at, slot):
            upper_ref[slot, 0:width, :] = nn(low_ref[0:width, :], up_ref[at]) + bias_ref[at, 6:7, :]
            grad_ref[slot, 0:width, :] = nt(gl_ref[0:width, :], down_ref[at])

        def bend(at, slot):
            upper = upper_ref[slot, 0:width, :]
            half = 0.5 * (1.0 + lax.erf(upper * 0.7071067811865476))
            density = jnp.exp(-0.5 * upper * upper) * 0.3989422804014327
            act_ref[at, 0:width, :] = (upper * half).astype(bf16)
            slope = half + upper * density
            gu_ref[at, 0:width, :] = (grad_ref[slot, 0:width, :] * slope).astype(bf16)

        def mix(at):
            down_acc[0:width, :] += nn(act_ref[at, 0:width, :], down_ref[at])
            gn_acc[0:width, :] += nt(gu_ref[at, 0:width, :], up_ref[at])

        lead(0, 0)
        for at in range(shards):
            if at + 1 < shards:
                lead(at + 1, (at + 1) % 2)
            bend(at, at % 2)
            if at > 0:
                mix(at - 1)
        mix(shards - 1)
        down_proj = down_acc[0:width, :]
        grad_normed = gn_acc[0:width, :]
        up_total[...] += tn(low_ref[0:width, :], gu_ref[place, 0:width, :])
        down_total[...] += tn(act_ref[place, 0:width, :], gl_ref[0:width, :])
        sums_ref[4:5, :] += jnp.sum(gu_ref[place, 0:width, :].astype(f32), axis=0, keepdims=True)
        result = jnp.where(valid, hidden + down_proj + rows_ref[5:6, :], 0.0)
        out_ref[0:width, :] = result.astype(bf16)
        grad_hidden = grad_result + norm_grad(grad_normed, xhat, inverse, rows_ref[3:4, :])
        grad_hidden_ref[0:width, :] = grad_hidden
        sums_ref[0:1, :] += jnp.sum(grad_normed * xhat, axis=0, keepdims=True)
        sums_ref[1:2, :] += jnp.sum(grad_normed, axis=0, keepdims=True)
        sums_ref[2:3, :] += jnp.sum(grad_hidden, axis=0, keepdims=True)
        sums_ref[3:4, :] += jnp.sum(grad_result, axis=0, keepdims=True)
        if width < PAGE:
            out_ref[width:PAGE, :] = jnp.zeros((PAGE - width, hidden.shape[1]), bf16)
            grad_hidden_ref[width:PAGE, :] = jnp.zeros((PAGE - width, hidden.shape[1]), f32)

    by_halves(count, body)

    @pl.when(page == pl.num_programs(0) - 1)
    def _():
        grad_up_ref[...] = up_total[...].astype(bf16)
        grad_down_ref[...] = down_total[...].astype(bf16)


def reduce_steps(bits, parts, sums, smalls, scratch):
    arrays = len(parts)
    got_core, got_one, got_two, got_more, kept_core, kept_one, send_sem, recv_sem = scratch[0:8]
    place = lax.axis_index("tensor")
    lane = lax.axis_index("dp")
    core, side_x, side_y, to_core, to_x, to_y = neighbours(lane)
    steps = [to_core, to_x, to_y]
    for bit in range(3, bits):
        size = 2**bit
        steps.append(size - 2 * size * ((lane // size) % 2))
    rows = parts[0].shape[0]
    quarter, eighth, sixteenth = rows // 4, rows // 8, rows // 16
    order = ((side_x, side_y, to_x, to_y), (side_y, side_x, to_y, to_x))
    sides = range(2)

    def device(step):
        return {"dp": lane + step, "tensor": place}

    def remote(stage, array, side, source, target, step):
        return pltpu.make_async_remote_copy(
            src_ref=source,
            dst_ref=target,
            send_sem=send_sem.at[stage, array, side],
            recv_sem=recv_sem.at[stage, array, side],
            device_id=device(step),
            device_id_type=pl.DeviceIdType.MESH,
        )

    def span(side, of_core, one=None, two=None):
        start = side * (rows // 2) + of_core * quarter
        if one is None:
            return pl.ds(pl.multiple_of(start, 16), quarter)
        start = start + one * eighth
        if two is None:
            return pl.ds(pl.multiple_of(start, 16), eighth)
        return pl.ds(pl.multiple_of(start + two * sixteenth, 16), sixteenth)

    def part_of(index, size):
        return pl.ds(pl.multiple_of(index * size, 16), size)

    def core_copy(array, side):
        return remote(0, array, side, parts[array].at[span(side, 1 - core)], got_core.at[array, side], to_core)

    def one_copy(array, side):
        one, two, to_one, to_two = order[side]
        source = kept_core.at[array, side, part_of(1 - one, eighth)]
        return remote(1, array, side, source, got_one.at[array, side], to_one)

    def two_copy(array, side):
        one, two, to_one, to_two = order[side]
        source = kept_one.at[array, side, part_of(1 - two, sixteenth)]
        return remote(2, array, side, source, got_two.at[array, side], to_two)

    def more_copy(array, side, bit):
        source = got_more.at[bit - 3, array, side]
        return remote(bit + 3, array, side, source, got_more.at[bits - 3 + bit - 3, array, side], steps[bit])

    def back_copy(stage, array, side, inward):
        one, two, to_one, to_two = order[side]
        if stage == 3:
            region, step = span(side, core, one, 1 - two if inward else two), to_two
        elif stage == 4:
            region, step = span(side, core, 1 - one if inward else one), to_one
        else:
            region, step = span(side, 1 - core if inward else core), to_core
        ref = sums[array].at[region]
        return remote(stage, array, side, ref, ref, step)

    def enter():
        greet([(lane + step, place) for step in steps])

    def begin():
        for array in range(arrays):
            for side in sides:
                core_copy(array, side).start()

    def add_core(array):
        for side in sides:
            keep = span(side, core)
            core_copy(array, side).wait_recv()
            kept_core[array, side] = (
                parts[array][keep, :].astype(f32) + got_core[array, side].astype(f32)
            ).astype(bf16)
            one_copy(array, side).start()

    def add_one(array):
        for side in sides:
            one, two, to_one, to_two = order[side]
            one_copy(array, side).wait_recv()
            kept_one[array, side] = (
                kept_core[array, side, part_of(one, eighth), :].astype(f32) + got_one[array, side].astype(f32)
            ).astype(bf16)
            two_copy(array, side).start()

    def add_two(array):
        for side in sides:
            one, two, to_one, to_two = order[side]
            two_copy(array, side).wait_recv()
            total = (
                kept_one[array, side, part_of(two, sixteenth), :].astype(f32) + got_two[array, side].astype(f32)
            ).astype(bf16)
            for bit in range(3, bits):
                got_more[bit - 3, array, side] = total
                more_copy(array, side, bit).start()
                more_copy(array, side, bit).wait()
                total = (total.astype(f32) + got_more[bits - 3 + bit - 3, array, side].astype(f32)).astype(bf16)
            sums[array][span(side, core, one, two), :] = total
            back_copy(3, array, side, False).start()

    def back(stage, array):
        for side in sides:
            back_copy(stage, array, side, True).wait_recv()
            if stage < 5:
                back_copy(stage + 1, array, side, False).start()

    def small_copy(index, bit):
        got, small_send, small_recv = scratch[8:11]
        source = smalls[index] if bit == 0 else got.at[index, bits + bit - 1]
        return pltpu.make_async_remote_copy(
            src_ref=source,
            dst_ref=got.at[index, bit],
            send_sem=small_send.at[index, bit],
            recv_sem=small_recv.at[index, bit],
            device_id=device(steps[bit]),
            device_id_type=pl.DeviceIdType.MESH,
        )

    def small_begin():
        for index in range(len(smalls)):
            small_copy(index, 0).start()

    def small_step(bit):
        got = scratch[8]
        for index in range(len(smalls)):
            small_copy(index, bit).wait()
            before = smalls[index][...] if bit == 0 else got[index, bits + bit - 1]
            got[index, bits + bit] = before + got[index, bit]
            if bit + 1 < bits:
                small_copy(index, bit + 1).start()

    def drain():
        for array in range(arrays):
            for side in sides:
                core_copy(array, side).wait_send()
                one_copy(array, side).wait_send()
                two_copy(array, side).wait_send()
                for stage in (3, 4, 5):
                    back_copy(stage, array, side, False).wait_send()

    ticks = (
        [functools.partial(add_core, array) for array in range(arrays)]
        + [functools.partial(add_one, array) for array in range(arrays)]
        + [functools.partial(add_two, array) for array in range(arrays)]
        + [functools.partial(back, stage, array) for stage in (3, 4, 5) for array in range(arrays)]
    )
    return enter, begin, ticks, drain, small_begin, small_step


def reduce_scratch(arrays, rows, model, bits):
    more = max(2 * (bits - 3), 1)
    return [
        pltpu.VMEM((arrays, 2, rows // 4, model), bf16),
        pltpu.VMEM((arrays, 2, rows // 8, model), bf16),
        pltpu.VMEM((arrays, 2, rows // 16, model), bf16),
        pltpu.VMEM((more, arrays, 2, rows // 16, model), bf16),
        pltpu.VMEM((arrays, 2, rows // 4, model), bf16),
        pltpu.VMEM((arrays, 2, rows // 8, model), bf16),
        pltpu.SemaphoreType.DMA((bits + 3, arrays, 2)),
        pltpu.SemaphoreType.DMA((bits + 3, arrays, 2)),
    ]


def backward_kernel(
    shards,
    bits,
    pages_here,
    x_ref,
    box_x_ref,
    box_y_ref,
    rows_ref,
    grad_hidden_ref,
    qkv_ref,
    probs_ref,
    inverse_ref,
    context_ref,
    gathered_ref,
    part_up_ref,
    part_down_ref,
    grad_input_ref,
    grad_pack_ref,
    sums_ref,
    grad_up_ref,
    grad_down_ref,
    weights,
    copy_sem,
    grad_qkv,
    grad_context,
    grad_probs,
    small_scores,
    pack_total,
    bias_total,
    levels_total,
    summed,
    *scratch,
):
    page = pl.program_id(0)
    pages = pl.num_programs(0)
    steps_here = pages_here
    place = lax.axis_index("tensor")
    width, model = x_ref.shape
    heads = model // HEAD_DIM
    own = model // shards
    own_heads = heads // shards
    bins = 64
    enter, begin, ticks, drain, _, _ = reduce_steps(
        bits, (part_up_ref, part_down_ref), (summed.at[0], summed.at[1]), (), scratch
    )
    weight_copies = [
        pltpu.make_async_copy(gathered_ref.at[:, pl.ds(kind * own, own)], weights.at[kind], copy_sem.at[kind])
        for kind in range(4)
    ]
    stores = [
        pltpu.make_async_copy(summed.at[index], target, copy_sem.at[4 + index])
        for index, target in enumerate((grad_up_ref, grad_down_ref))
    ]

    @pl.when(page == 0)
    def _():
        for copy in weight_copies:
            copy.start()
        enter()
        begin()
        pack_total[...] = jnp.zeros_like(pack_total)
        bias_total[...] = jnp.zeros_like(bias_total)
        levels_total[...] = jnp.zeros_like(levels_total)
        sums_ref[...] = jnp.zeros_like(sums_ref)
        for copy in weight_copies:
            copy.wait()

    points = 5

    def point(index):
        for at, act in enumerate(ticks):
            where = (at + 1) * points * steps_here // (len(ticks) + 1) - 1
            if where % points == index:
                pl.when(page == where // points)(act)

    grad_hidden = grad_hidden_ref[...]
    grad_low = grad_hidden.astype(bf16)
    grad_context[...] = nt(weights[3].reshape(model, model), grad_low)
    hot = one_hot_columns(box_x_ref, box_y_ref, bins)
    back_hot = one_hot_columns(box_x_ref, box_y_ref, bins, True)

    def order(at):
        return lax.rem(place * own_heads + at, heads)

    def rows_of(at):
        return pl.ds(pl.multiple_of(order(at) * HEAD_DIM, HEAD_DIM), HEAD_DIM)

    def lead(at):
        rows = rows_of(at)
        grad_mixed = (grad_context[rows] * inverse_ref[0, order(at)]).astype(bf16)
        grad_probs[at % 2] = tn(qkv_ref[0, 2, rows], grad_mixed)
        delta = jnp.sum(
            grad_mixed.astype(f32) * context_ref[0, rows].astype(f32), axis=0, keepdims=True
        )
        return grad_mixed, delta

    def soften(at, delta):
        probs = probs_ref[0, order(at)].astype(f32)
        small_scores[at % 2] = (probs * (grad_probs[at % 2] - delta)).astype(bf16)

    def mix(at, grad_mixed):
        rows = rows_of(at)
        query = qkv_ref[0, 0, rows]
        key = qkv_ref[0, 1, rows]
        grad_scores = small_scores[at % 2]
        grad_value = nt(grad_mixed, probs_ref[0, order(at)])
        grad_key = nt(query, grad_scores) * LN2
        both = nn(jnp.concatenate([key, hot], axis=0) if at < own_heads else key, grad_scores)
        grad_qkv[0, rows] = (both[0:HEAD_DIM] * HEAD_DIM**-0.5).astype(bf16)
        grad_qkv[1, rows] = grad_key.astype(bf16)
        grad_qkv[2, rows] = grad_value.astype(bf16)
        if at < own_heads:
            levels_total[at] += nt(both[HEAD_DIM:].astype(bf16), back_hot)

    point(0)
    kept = [lead(0)]
    for at in range(heads):
        if at + 1 < heads:
            kept.append(lead(at + 1))
        soften(at, kept[at][1])
        if at > 0:
            mix(at - 1, kept[at - 1][0])
        if at % 3 == 2 and at + 1 < heads:
            point(1 + at // 3)
    mix(heads - 1, kept[-1][0])
    point(4)
    tokens = x_ref[...].astype(f32)
    xhat, inverse = norm_parts(tokens)
    low = (xhat * rows_ref[0:1, :] + rows_ref[1:2, :]).astype(bf16)
    mine = pl.ds(pl.multiple_of(place * own, own), own)
    stacked = jnp.concatenate([grad_qkv[kind, mine] for kind in range(3)], axis=0)
    pack_total[0 : 3 * own, :] += nn(stacked, low)
    pack_total[3 * own :, :] += nn(context_ref[0, mine], grad_low)
    wide = stacked.astype(f32)
    folded = wide[:, 0:BLOCK]
    for at in range(1, width // BLOCK):
        folded = folded + wide[:, at * BLOCK : (at + 1) * BLOCK]
    bias_total[...] += folded
    grad_normed = tn(grad_qkv[0], weights[0].reshape(model, model))
    for kind in (1, 2):
        grad_normed = grad_normed + tn(grad_qkv[kind], weights[kind].reshape(model, model))
    grad_total = grad_hidden + norm_grad(grad_normed, xhat, inverse, rows_ref[0:1, :])
    grad_input_ref[...] = grad_total.astype(bf16)
    sums_ref[0:1, :] += jnp.sum(grad_normed * xhat, axis=0, keepdims=True)
    sums_ref[1:2, :] += jnp.sum(grad_normed, axis=0, keepdims=True)

    @pl.when(page == pages - 1)
    def _():
        grad_pack_ref[...] = pack_total[...].astype(bf16)
        row = jnp.sum(bias_total[...].T, axis=0, keepdims=True)
        sums_ref[2:3, 0:own] = row[:, 0:own]
        sums_ref[3:4, 0:own] = row[:, 2 * own : 3 * own]
        lane = lax.broadcasted_iota(jnp.int32, (bins, 2 * bins), 1)
        for one in range(own_heads):
            for kind in range(2):
                block = levels_total[one, kind * bins : (kind + 1) * bins, :]
                inside = lane >= bins if kind else lane < bins
                rolled = pltpu.roll(jnp.where(inside, block, 0.0), kind * bins, 1, stride=1, stride_axis=0)
                at = (kind * own_heads + one) * 2 * bins
                sums_ref[4:5, at : at + 2 * bins] = jnp.sum(rolled, axis=0, keepdims=True)
        for copy in stores:
            copy.start()
        drain()
        for copy in stores:
            copy.wait()


def reduce_kernel(bits, part_ref, small_one_ref, small_two_ref, sum_ref, sum_one_ref, sum_two_ref, *scratch):
    enter, begin, ticks, drain, small_begin, small_step = reduce_steps(
        bits, (part_ref,), (sum_ref,), (small_one_ref, small_two_ref), scratch
    )
    enter()
    begin()
    small_begin()
    for at, act in enumerate(ticks):
        act()
        if at < 3:
            small_step(at)
    for bit in range(3, bits):
        small_step(bit)
    drain()
    sum_one_ref[...] = scratch[8][0, 2 * bits - 1]
    sum_two_ref[...] = scratch[8][1, 2 * bits - 1]


def finish_kernel(pack_ref, up_ref, down_ref, one_ref, two_ref, qkv, qv_bias, out, up, down, tables, rows):
    own = out.shape[0]
    bins = tables.shape[-1]
    for kind in range(3):
        qkv[kind] = pack_ref[kind * own : (kind + 1) * own, :].astype(f32)
    out[...] = pack_ref[3 * own :, :].astype(f32)
    up[...] = up_ref[...].astype(f32)
    down[...] = down_ref[...].astype(f32)
    qv_bias[...] = one_ref[2:4, 0:own]
    rows[0:2, :] = one_ref[0:2, :]
    rows[2:7, :] = two_ref[0:5, :]
    rows[7:8, :] = one_ref[7:8, :]
    m = lax.broadcasted_iota(jnp.int32, (2 * bins, bins), 0)
    level = lax.broadcasted_iota(jnp.int32, (2 * bins, bins), 1)
    pick = jnp.where(jnp.clip(m - (bins - 1), -(bins // 2), bins // 2 - 1) + bins // 2 == level, 1.0, 0.0)
    own_heads = tables.shape[0]
    for one in range(own_heads):
        for kind in range(2):
            at = (kind * own_heads + one) * 2 * bins
            line = jnp.broadcast_to(one_ref[4:5, at : at + 2 * bins], (8, 2 * bins))
            folded = lax.dot_general(
                line, pick, (((1,), (0,)), ((), ())), precision=lax.Precision.HIGHEST, preferred_element_type=f32
            )
            tables[one, kind : kind + 1, :] = folded[0:1]


ANYWHERE = pl.BlockSpec(memory_space=pl.ANY)
IN_VMEM = pl.BlockSpec(memory_space=pltpu.VMEM)


def whole(shape):
    return pl.BlockSpec(shape, lambda *_: (0,) * len(shape), pipeline_mode=pl.Buffered(1))


def page_rows(model):
    return pl.BlockSpec((PAGE, model), lambda p, *_: (p, 0))


def page_block(*shape):
    return pl.BlockSpec((1,) + shape, lambda p, *_: (p,) + (0,) * len(shape))


def params(collective_id=None):
    if collective_id is None:
        return pltpu.CompilerParams(vmem_limit_bytes=VMEM_LIMIT)
    return pltpu.CompilerParams(
        vmem_limit_bytes=VMEM_LIMIT, collective_id=collective_id, has_side_effects=True
    )


def attention_forward(shards, counts, inputs, keep, box_x, box_y, rows, bias, tables, qkv_weight, out_weight, up, down):
    rows_here, model = inputs.shape
    pages = rows_here // PAGE
    own = model // shards
    bins = tables.shape[-1]
    heads = model // HEAD_DIM
    gathered = jax.ShapeDtypeStruct((shards,) + up.shape, bf16)
    return pl.pallas_call(
        functools.partial(forward_kernel, shards),
        out_shape=(
            jax.ShapeDtypeStruct((pages, 3, model, PAGE), bf16),
            jax.ShapeDtypeStruct((pages, heads, PAGE, PAGE), bf16),
            jax.ShapeDtypeStruct((pages, heads, 1, PAGE), f32),
            jax.ShapeDtypeStruct((pages, model, PAGE), bf16),
            jax.ShapeDtypeStruct((rows_here, model), f32),
            gathered,
            gathered,
            gathered,
            jax.ShapeDtypeStruct((shards,) + rows.shape, f32),
        ),
        grid_spec=pltpu.PrefetchScalarGridSpec(
            num_scalar_prefetch=1,
            grid=(pages,),
            in_specs=[page_rows(model)]
            + [page_block(1, PAGE)] * 3
            + [whole(rows.shape), whole(bias.shape), whole(tables.shape)]
            + [ANYWHERE] * 4,
            out_specs=(
                page_block(3, model, PAGE),
                page_block(heads, PAGE, PAGE),
                page_block(heads, 1, PAGE),
                page_block(model, PAGE),
                page_rows(model),
                ANYWHERE,
                ANYWHERE,
                ANYWHERE,
                ANYWHERE,
            ),
            scratch_shapes=[
                pltpu.VMEM((4, shards, own, model), bf16),
                pltpu.SemaphoreType.DMA((14,)),
                pltpu.VMEM((3,) + up.shape, bf16),
                pltpu.VMEM((shards,) + bias.shape, f32),
                pltpu.VMEM((shards,) + tables.shape, f32),
            ]
            + gather_semaphores(3, shards)
            + [
                pltpu.VMEM((2, model, 128), f32),
                pltpu.VMEM((heads * 2 * bins, 2 * bins), bf16),
                pltpu.VMEM((heads * 2 * bins, PAGE), bf16),
                pltpu.VMEM((2, PAGE, PAGE), f32),
            ],
        ),
        compiler_params=params(1),
        name="attention_forward",
    )(counts, inputs, keep, box_x, box_y, rows, bias, tables, qkv_weight, out_weight, up, down)


def feed_forward(counts, place, hidden, cotangent, rows, rows_all, up_all, down_all):
    rows_here, model = hidden.shape
    pages = rows_here // PAGE
    shards, _, hidden_units = up_all.shape
    return pl.pallas_call(
        mlp_kernel,
        out_shape=(
            jax.ShapeDtypeStruct((rows_here, model), bf16),
            jax.ShapeDtypeStruct((rows_here, model), f32),
            jax.ShapeDtypeStruct((model, hidden_units), bf16),
            jax.ShapeDtypeStruct((hidden_units, model), bf16),
            jax.ShapeDtypeStruct((8, model), f32),
        ),
        grid_spec=pltpu.PrefetchScalarGridSpec(
            num_scalar_prefetch=2,
            grid=(pages,),
            in_specs=[
                page_rows(model),
                page_rows(model),
                whole(rows.shape),
                whole(rows_all.shape),
                whole((shards, model, hidden_units)),
                whole((shards, hidden_units, model)),
            ],
            out_specs=(
                page_rows(model),
                page_rows(model),
                whole((model, hidden_units)),
                whole((hidden_units, model)),
                whole((8, model)),
            ),
            scratch_shapes=[
                pltpu.VMEM((model, hidden_units), f32),
                pltpu.VMEM((hidden_units, model), f32),
                pltpu.VMEM((PAGE, model), bf16),
                pltpu.VMEM((PAGE, model), bf16),
                pltpu.VMEM((PAGE, model), f32),
                pltpu.VMEM((PAGE, model), f32),
                pltpu.VMEM((shards, PAGE, hidden_units), bf16),
                pltpu.VMEM((shards, PAGE, hidden_units), bf16),
                pltpu.VMEM((2, PAGE, hidden_units), f32),
                pltpu.VMEM((2, PAGE, hidden_units), f32),
            ],
        ),
        compiler_params=params(),
        name="feed_forward",
    )(counts, place, hidden, cotangent, rows, rows_all, up_all, down_all)


def attention_backward(
    shards,
    devices,
    inputs,
    box_x,
    box_y,
    rows,
    grad_hidden,
    qkv,
    probs,
    inverse,
    context,
    gathered,
    part_up,
    part_down,
):
    rows_here, model = inputs.shape
    pages, heads = probs.shape[:2]
    own = model // shards
    bins = 64
    bits = devices.bit_length() - 1
    return pl.pallas_call(
        functools.partial(backward_kernel, shards, bits, pages),
        out_shape=(
            jax.ShapeDtypeStruct((rows_here, model), bf16),
            jax.ShapeDtypeStruct((4 * own, model), bf16),
            jax.ShapeDtypeStruct((8, model), f32),
            jax.ShapeDtypeStruct(part_up.shape, bf16),
            jax.ShapeDtypeStruct(part_down.shape, bf16),
        ),
        grid_spec=pltpu.PrefetchScalarGridSpec(
            num_scalar_prefetch=0,
            grid=(pages,),
            in_specs=[page_rows(model)]
            + [page_block(1, PAGE)] * 2
            + [whole(rows.shape)]
            + [
                page_rows(model),
                page_block(3, model, PAGE),
                page_block(heads, PAGE, PAGE),
                page_block(heads, 1, PAGE),
                page_block(model, PAGE),
                ANYWHERE,
                whole(part_up.shape),
                whole(part_down.shape),
            ],
            out_specs=(
                page_rows(model),
                whole((4 * own, model)),
                whole((8, model)),
                ANYWHERE,
                ANYWHERE,
            ),
            scratch_shapes=[
                pltpu.VMEM((4, shards, own, model), bf16),
                pltpu.SemaphoreType.DMA((6,)),
                pltpu.VMEM((3, model, PAGE), bf16),
                pltpu.VMEM((model, PAGE), f32),
                pltpu.VMEM((2, PAGE, PAGE), f32),
                pltpu.VMEM((2, PAGE, PAGE), bf16),
                pltpu.VMEM((4 * own, model), f32),
                pltpu.VMEM((3 * own, BLOCK), f32),
                pltpu.VMEM((own // HEAD_DIM, 2 * bins, 2 * bins), f32),
                pltpu.VMEM((2,) + part_up.shape, bf16),
            ]
            + reduce_scratch(2, part_up.shape[0], model, bits),
        ),
        compiler_params=params(2),
        name="attention_backward",
    )(
        inputs,
        box_x,
        box_y,
        rows,
        grad_hidden,
        qkv,
        probs,
        inverse,
        context,
        gathered,
        part_up,
        part_down,
    )


def reduce_grads(devices, part, small_one, small_two):
    rows, model = part.shape
    bits = devices.bit_length() - 1
    return pl.pallas_call(
        functools.partial(reduce_kernel, bits),
        out_shape=(jax.ShapeDtypeStruct(part.shape, bf16),)
        + tuple(jax.ShapeDtypeStruct(small.shape, f32) for small in (small_one, small_two)),
        in_specs=[IN_VMEM] * 3,
        out_specs=(IN_VMEM,) * 3,
        scratch_shapes=reduce_scratch(1, rows, model, bits)
        + [
            pltpu.VMEM((2, 2 * bits) + small_one.shape, f32),
            pltpu.SemaphoreType.DMA((2, bits)),
            pltpu.SemaphoreType.DMA((2, bits)),
        ],
        compiler_params=params(3),
        name="reduce_grads",
    )(part, small_one, small_two)


def finish_grads(pack, up, down, small_one, small_two, bins):
    own, model = pack.shape[0] // 4, pack.shape[1]
    return pl.pallas_call(
        finish_kernel,
        out_shape=(
            jax.ShapeDtypeStruct((3, own, model), f32),
            jax.ShapeDtypeStruct((2, own), f32),
            jax.ShapeDtypeStruct((own, model), f32),
            jax.ShapeDtypeStruct(up.shape, f32),
            jax.ShapeDtypeStruct(down.shape, f32),
            jax.ShapeDtypeStruct((own // HEAD_DIM, 2, bins), f32),
            jax.ShapeDtypeStruct(small_one.shape, f32),
        ),
        in_specs=[IN_VMEM] * 5,
        out_specs=(IN_VMEM,) * 7,
        compiler_params=params(),
        name="finish_grads",
    )(pack, up, down, small_one, small_two)


def on_device(
    inputs,
    cotangent,
    counts,
    keep_mask,
    box_x,
    box_y,
    gain_one,
    shift_one,
    w_qkv,
    b_qv,
    w_out,
    b_out,
    gain_two,
    shift_two,
    w_up,
    b_up,
    w_down,
    b_down,
    rel_tables,
    *,
    devices,
):
    rows_here, model = inputs.shape
    pages = rows_here // PAGE
    own_heads, bins = rel_tables.shape[1:]
    own = own_heads * HEAD_DIM
    shards = model // own
    place = lax.axis_index("tensor").astype(jnp.int32).reshape(1)
    paged = lambda array: array.reshape(pages, 1, PAGE)
    keep_mask, box_x, box_y = paged(keep_mask), paged(box_x), paged(box_y)
    rows = jnp.concatenate([gain_one, shift_one, b_out, gain_two, shift_two, b_down, b_up, b_up]).reshape(8, model)

    qkv, probs, inverse, context, hidden, gathered, up_all, down_all, rows_all = attention_forward(
        shards,
        counts,
        inputs,
        keep_mask,
        box_x,
        box_y,
        rows,
        b_qv,
        rel_tables.transpose(1, 0, 2),
        w_qkv.transpose(0, 2, 1).reshape(3 * own, model),
        w_out,
        w_up,
        w_down,
    )
    out, grad_hidden, part_up, part_down, small_two = feed_forward(
        counts, place, hidden, cotangent, rows, rows_all, up_all, down_all
    )
    grad_input, part_pack, small_one, grad_up, grad_down = attention_backward(
        shards,
        devices,
        inputs,
        box_x,
        box_y,
        rows,
        grad_hidden,
        qkv,
        probs,
        inverse,
        context,
        gathered,
        part_up,
        part_down,
    )
    grad_pack, small_one, small_two = reduce_grads(devices, part_pack, small_one, small_two)
    grad_qkv, grad_b_qv, grad_w_out, grad_w_up, grad_w_down, grad_tables, sums = finish_grads(
        grad_pack, grad_up, grad_down, small_one, small_two, bins
    )
    return (
        out,
        grad_input,
        grad_qkv.transpose(0, 2, 1),
        grad_b_qv,
        grad_w_out,
        sums[4],
        sums[0],
        sums[1],
        sums[2],
        sums[3],
        grad_w_up,
        sums[6],
        grad_w_down,
        sums[5],
        grad_tables.transpose(1, 0, 2),
    )


def solution(mesh):
    placed = (
        P("dp", None),
        P("dp", None),
        P("dp"),
        P("dp"),
        P("dp"),
        P("dp"),
        P(),
        P(),
        P(None, None, "tensor"),
        P(None, "tensor"),
        P("tensor", None),
        P(),
        P(),
        P(),
        P(None, "tensor"),
        P("tensor"),
        P("tensor", None),
        P(),
        P(None, "tensor", None),
    )
    return jax.shard_map(
        functools.partial(on_device, devices=mesh.shape["dp"]),
        mesh=mesh,
        in_specs=placed,
        out_specs=(
            P("dp", None),
            P("dp", None),
            P(None, None, "tensor"),
            P(None, "tensor"),
            P("tensor", None),
            P(),
            P(),
            P(),
            P(),
            P(),
            P(None, "tensor"),
            P("tensor"),
            P("tensor", None),
            P(),
            P(None, "tensor", None),
        ),
        check_vma=False,
    )
```

profile of v0, /device:TPU:0, one launch (start us, length us, event | category | flops | bytes accessed | tf_op | source)
XLA Modules:
  0.0 261.5 jit_solution(15721958508131994288)
XLA Ops:
  0.7 0.7 constant_dynamic-update-slice_fusion.7
  1.4 0.7 constant_dynamic-update-slice_fusion.6
  2.0 0.7 constant_dynamic-update-slice_fusion.5
  2.7 0.7 constant_dynamic-update-slice_fusion.4
  3.4 0.7 constant_dynamic-update-slice_fusion.3
  4.1 0.7 constant_dynamic-update-slice_fusion.2
  4.8 0.7 constant_dynamic-update-slice_fusion.1
  5.5 0.7 constant_dynamic-update-slice_fusion
  6.2 0.6 reshape.52.rows_ref
  6.8 97.2 %attention_forward.1 = (bf16[4,3,768,512]{3,2,1,0:T(8,128)(2,1)}, bf16[4,12,512,512]{3,2,1,0:T(8,128)(2,1)}, f32[4,12,1,512]{3,2,1,0:T(1,128)}, bf16[4,768,512]{...) custom-call(s32[4]{0:T(128)} %counts_ref.3, ...), custom_call_target="tpu_custom_call" | custom-call | tf_op jit(solution)/shard_map/attention_forward/pallas_call | solution.py:907
  104.0 59.1 %feed_forward.1 = (bf16[2048,768]{1,0:T(8,128)(2,1)}, f32[2048,768]{1,0:T(8,128)}, bf16[768,768]{1,0:T(8,128)(2,1)}, bf16[768,768]{1,0:T(8,128)(2,1)}, f32[8,768]{1,0:T(8,128)}) custom-call(s32[4]{0:T(128)} %counts_ref.3, s32[1]{0:T(128)} %bitcast.place_ref, f32[2048,768]{1,0:T(8,128)} %get-tuple-element.44.hidden_ref, bf16[2048,768]{1,0:T(8,128)(2,1)} %cotangent_ref.1, ...), custom_call_target="tpu_custom_call" | custom-call | tf_op jit(solution)/shard_map/feed_forward/pallas_call | solution.py:962
  163.1 66.4 %attention_backward.1 = (bf16[2048,768]{1,0:T(8,128)(2,1)}, bf16[768,768]{1,0:T(8,128)(2,1)}, f32[8,768]{1,0:T(8,128)}, bf16[768,768]{1,0:T(8,128)(2,1)}, bf16[768,768]{1,0:T(8,128)(2,1)}) custom-call(bf16[2048,768]{1,0:T(8,128)(2,1)} %x_ref.3, s32[4,1,512]{2,1,0:T(1,128)} %bitcast.12, s32[4,1,512]{2,1,0:T(1,128)} %bitcast.14, f32[8,768]{1,0:T(8,128)} %reshape.52.rows_ref, ...), custom_call_target="tpu_custom_call" | custom-call | tf_op jit(solution)/shard_map/attention_backward/pallas_call | solution.py:1028
  229.5 0.0 copy-start
  229.5 23.3 %reduce_grads.1 = (bf16[768,768]{1,0:T(8,128)(2,1)}, f32[8,768]{1,0:T(8,128)}, f32[8,768]{1,0:T(8,128)}) custom-call(bf16[768,768]{1,0:T(8,128)(2,1)} %get-tuple-element.58.part_ref, f32[8,768]{1,0:T(8,128)} %get-tuple-element.59.small_one_ref, f32[8,768]{1,0:T(8,128)} %get-tuple-element.60.small_two_ref), custom_call_target="tpu_custom_call" | custom-call | tf_op jit(solution)/shard_map/reduce_grads/pallas_call | solution.py:1095
  252.8 5.4 %finish_grads.1 = (f32[3,192,768]{2,1,0:T(8,128)}, f32[2,192]{1,0:T(2,128)}, f32[192,768]{1,0:T(8,128)}, f32[768,768]{1,0:T(8,128)}, f32[768,768]{1,0:T(8,128)}, /*index=5*/f32[3,2,64]{2,1,0:T(2,128)}, f32[8,768]{1,0:T(8,128)}) custom-call(bf16[768,768]{1,0:T(8,128)(2,1)} %get-tuple-element.61.pack_ref, bf16[768,768]{1,0:T(8,128)(2,1)} %get-tuple-element.62.up_ref, ...), custom_call_target="tpu_custom_call" | custom-call | tf_op jit(solution)/shard_map/finish_grads/pallas_call | solution.py:1114
  258.2 1.7 slice_reduce_fusion
  259.9 0.0 copy-done
  259.9 1.7 copy.43
  (1 shorter events, 0.0 us)
Async XLA Ops:
  229.5 30.4 %copy-start = (bf16[2048,768]{1,0:T(8,128)(2,1)S(1)}, bf16[2048,768]{1,0:T(8,128)(2,1)}, u32[]{:S(2)}) copy-start(bf16[2048,768]{1,0:T(8,128)(2,1)} %get-tuple-element.96) | copy-start | bytes 9437188
where the time goes:
time: 262 us
  Pallas kernels  251 us (96%)
  local copies, waits for them, and re-layouts  9.49 us (4%)
    pallas_call x1, Pallas kernels, attention_forward(): pl.pallas_call(functools.partial(forward_kernel, shards), out_shape=(jax....  97.2 us
    pallas_call x1, Pallas kernels, attention_backward(): pl.pallas_call(functools.partial(backward_kernel, shards, bits, pages), o...  66.4 us
    pallas_call x1, Pallas kernels, feed_forward(): pl.pallas_call(mlp_kernel, out_shape=(jax.ShapeDtypeStruct((rows_here, mo...  59.1 us
    pallas_call x1, Pallas kernels, reduce_grads(): pl.pallas_call(functools.partial(reduce_kernel, bits), out_shape=(jax.Sha...  23.3 us
    unnamed x10, local copies, waits for them, and re-layouts  6.52 us
    pallas_call x1, Pallas kernels, finish_grads(): pl.pallas_call(finish_kernel, out_shape=(jax.ShapeDtypeStruct((3, own, mo...  5.4 us

commit v1 on v0

--- a/solution.py
+++ b/solution.py
@@ -187,12 +187,30 @@
     items = [(array, hop) for array in range(arrays) for hop in hops]
     stages = (arrive, spread_near, spread_far, finish)
 
-    def tick(at):
-        for stage, act in enumerate(stages):
-            if 0 <= at - stage < len(items):
-                act(*items[at - stage])
-
-    return enter, begin, tick, len(items) + len(stages) - 1, drain
+    def act(stage, item):
+        stages[stage](*items[item])
+
+    return enter, begin, act, len(items), drain
+
+
+def gather_order(items, first):
+    start = []
+    for tick in range(first + 2):
+        for stage in (0, 1, 2):
+            if 0 <= tick - stage < first:
+                start.append((stage, tick - stage))
+            elif stage == 0 and tick < min(items, first + 2):
+                later = (stage, tick)
+                start.append(later)
+    start += [(3, item) for item in range(first)]
+    ready = first + 2
+    groups = []
+    for tick in range(first + 1, items + 3):
+        group = [(stage, tick - stage) for stage in (3, 2, 1) if first <= tick - stage < items]
+        if ready <= tick + 1 < items:
+            group.append((0, tick + 1))
+        groups.append(group)
+    return start, groups
 
 
 def gather_semaphores(arrays, shards):
@@ -206,7 +224,13 @@
     keep_ref,
     box_x_ref,
     box_y_ref,
-    rows_ref,
+    gain_one_ref,
+    shift_one_ref,
+    out_bias_ref,
+    gain_two_ref,
+    shift_two_ref,
+    down_bias_ref,
+    up_bias_ref,
     bias_ref,
     tables_ref,
     qkv_weight_ref,
@@ -221,7 +245,9 @@
     gathered_ref,
     up_all_ref,
     down_all_ref,
+    rows_ref,
     rows_all_ref,
+    rows,
     weights,
     copy_sem,
     bounce,
@@ -243,8 +269,8 @@
     own_heads = heads // shards
     bins = tables_ref.shape[-1]
     split = qkv_weight_ref.shape[0]
-    smalls, small_targets = (rows_ref, bias_ref, tables_ref), (rows_all_ref, bias_all, tables_all)
-    enter, begin, tick, ticks, drain = gather_steps(
+    smalls, small_targets = (rows, bias_ref, tables_ref), (rows_all_ref, bias_all, tables_all)
+    enter, begin, act, items, drain = gather_steps(
         shards,
         (bounce.at[0], up_ref, down_ref),
         (gathered_ref, up_all_ref, down_all_ref),
@@ -272,12 +298,26 @@
         )
         for kind in range(4)
     ]
-    before = shards - 1 + 3
+    start, groups = gather_order(items, shards - 1)
 
     @pl.when(page == 0)
     def _():
         for copy in loads:
             copy.start()
+        vectors = (
+            gain_one_ref,
+            shift_one_ref,
+            out_bias_ref,
+            gain_two_ref,
+            shift_two_ref,
+            down_bias_ref,
+            up_bias_ref,
+            up_bias_ref,
+        )
+        for index, vector in enumerate(vectors):
+            for part in range(model // 128):
+                rows[index : index + 1, part * 128 : (part + 1) * 128] = vector[part : part + 1, :]
+        rows_ref[...] = rows[...]
         enter()
         for copy in loads[0:2]:
             copy.wait()
@@ -286,18 +326,18 @@
             copy.wait()
         for copy in stores:
             copy.start()
+        for stage, item in start:
+            act(stage, item)
         for copy in stores:
             copy.wait()
-        for at in range(before):
-            tick(at)
         for copy in weight_copies:
             copy.start()
         drain(True)
         for shard in range(shards):
-            rows = slice(shard * own, (shard + 1) * own)
+            span = slice(shard * own, (shard + 1) * own)
             for kind in range(2):
                 wide = jnp.broadcast_to(bias_all[shard, kind : kind + 1, :], (128, own))
-                bias_columns[kind, rows, :] = wide.T
+                bias_columns[kind, span, :] = wide.T
         m = lax.broadcasted_iota(jnp.int32, (bins, 2 * bins), 1)
         signed = jnp.where(m >= bins, 2 * bins - m, -m)
         level = lax.broadcasted_iota(jnp.int32, (bins, 2 * bins), 0)
@@ -316,17 +356,20 @@
             copy.wait()
 
     points = 5
-    left = ticks - before
+
+    def run_group(group):
+        for stage, item in group:
+            act(stage, item)
 
     def point(index):
-        for at in range(before, ticks):
-            where = (at - before + 1) * points * pages // (left + 1) - 1
+        for at, group in enumerate(groups):
+            where = (at + 1) * points * pages // (len(groups) + 1) - 1
             if where % points == index:
-                pl.when(page == where // points)(functools.partial(tick, at))
+                pl.when(page == where // points)(functools.partial(run_group, group))
 
     tokens = x_ref[...].astype(f32)
     xhat, _ = norm_parts(tokens)
-    low = (xhat * rows_ref[0:1, :] + rows_ref[1:2, :]).astype(bf16)
+    low = (xhat * rows[0:1, :] + rows[1:2, :]).astype(bf16)
     for kind in range(3):
         product = nt(weights[kind].reshape(model, model), low)
         if kind == 0:
@@ -346,9 +389,9 @@
     eye = lax.broadcasted_iota(jnp.int32, (BLOCK, BLOCK), 0) == lax.broadcasted_iota(jnp.int32, (BLOCK, BLOCK), 1)
 
     def score(index, slot):
-        rows = slice(index * HEAD_DIM, (index + 1) * HEAD_DIM)
-        query = qkv_ref[0, 0, rows]
-        key = qkv_ref[0, 1, rows]
+        span = slice(index * HEAD_DIM, (index + 1) * HEAD_DIM)
+        query = qkv_ref[0, 0, span]
+        key = qkv_ref[0, 1, span]
         bias = spread[index * 2 * bins : (index + 1) * 2 * bins, :]
         left = jnp.concatenate([key, key_pad, hot], axis=0)
         right = jnp.concatenate([query, query_pad, bias], axis=0)
@@ -365,11 +408,11 @@
         probs_ref[0, index] = jnp.exp2(scores[slot] - top).astype(bf16)
 
     def mix(index):
-        rows = slice(index * HEAD_DIM, (index + 1) * HEAD_DIM)
-        mixed = nn(jnp.concatenate([qkv_ref[0, 2, rows], ones], axis=0), probs_ref[0, index])
+        span = slice(index * HEAD_DIM, (index + 1) * HEAD_DIM)
+        mixed = nn(jnp.concatenate([qkv_ref[0, 2, span], ones], axis=0), probs_ref[0, index])
         inverse = 1.0 / mixed[HEAD_DIM : HEAD_DIM + 1]
         inverse_ref[0, index] = inverse
-        context_ref[0, rows] = (mixed[0:HEAD_DIM] * inverse).astype(bf16)
+        context_ref[0, span] = (mixed[0:HEAD_DIM] * inverse).astype(bf16)
 
     point(0)
     owns = [score(0, 0)]
@@ -384,7 +427,7 @@
     mix(heads - 1)
     point(4)
     attended = tn(context_ref[0], weights[3].reshape(model, model))
-    hidden_ref[...] = tokens + attended + rows_ref[2:3, :]
+    hidden_ref[...] = tokens + attended + rows[2:3, :]
 
     @pl.when(page == pages - 1)
     def _():
@@ -897,7 +940,7 @@
     )
 
 
-def attention_forward(shards, counts, inputs, keep, box_x, box_y, rows, bias, tables, qkv_weight, out_weight, up, down):
+def attention_forward(shards, counts, inputs, keep, box_x, box_y, vectors, bias, tables, qkv_weight, out_weight, up, down):
     rows_here, model = inputs.shape
     pages = rows_here // PAGE
     own = model // shards
@@ -915,14 +958,16 @@
             gathered,
             gathered,
             gathered,
-            jax.ShapeDtypeStruct((shards,) + rows.shape, f32),
+            jax.ShapeDtypeStruct((8, model), f32),
+            jax.ShapeDtypeStruct((shards, 8, model), f32),
         ),
         grid_spec=pltpu.PrefetchScalarGridSpec(
             num_scalar_prefetch=1,
             grid=(pages,),
             in_specs=[page_rows(model)]
             + [page_block(1, PAGE)] * 3
-            + [whole(rows.shape), whole(bias.shape), whole(tables.shape)]
+            + [whole(vector.shape) for vector in vectors]
+            + [whole(bias.shape), whole(tables.shape)]
             + [ANYWHERE] * 4,
             out_specs=(
                 page_block(3, model, PAGE),
@@ -933,9 +978,11 @@
                 ANYWHERE,
                 ANYWHERE,
                 ANYWHERE,
+                whole((8, model)),
                 ANYWHERE,
             ),
             scratch_shapes=[
+                pltpu.VMEM((8, model), f32),
                 pltpu.VMEM((4, shards, own, model), bf16),
                 pltpu.SemaphoreType.DMA((14,)),
                 pltpu.VMEM((3,) + up.shape, bf16),
@@ -952,7 +999,7 @@
         ),
         compiler_params=params(1),
         name="attention_forward",
-    )(counts, inputs, keep, box_x, box_y, rows, bias, tables, qkv_weight, out_weight, up, down)
+    )(counts, inputs, keep, box_x, box_y, *vectors, bias, tables, qkv_weight, out_weight, up, down)
 
 
 def feed_forward(counts, place, hidden, cotangent, rows, rows_all, up_all, down_all):
@@ -1160,16 +1207,18 @@
     place = lax.axis_index("tensor").astype(jnp.int32).reshape(1)
     paged = lambda array: array.reshape(pages, 1, PAGE)
     keep_mask, box_x, box_y = paged(keep_mask), paged(box_x), paged(box_y)
-    rows = jnp.concatenate([gain_one, shift_one, b_out, gain_two, shift_two, b_down, b_up, b_up]).reshape(8, model)
-
-    qkv, probs, inverse, context, hidden, gathered, up_all, down_all, rows_all = attention_forward(
+    vectors = [
+        vector.reshape(-1, 128) for vector in (gain_one, shift_one, b_out, gain_two, shift_two, b_down, b_up)
+    ]
+
+    qkv, probs, inverse, context, hidden, gathered, up_all, down_all, rows, rows_all = attention_forward(
         shards,
         counts,
         inputs,
         keep_mask,
         box_x,
         box_y,
-        rows,
+        vectors,
         b_qv,
         rel_tables.transpose(1, 0, 2),
         w_qkv.transpose(0, 2, 1).reshape(3 * own, model),

time: 262 us -> 252 us (0.962)
  local copies, waits for them, and re-layouts: 9.49 us -> 3.34 us
  Pallas kernels: 251 us -> 247 us
    pallas_call x1, Pallas kernels: 97.2 us -> 92.3 us  [attention_forward(): pl.pallas_call(functools.partial(forward_kernel, shards), out_shape=(jax....]
    unnamed x10 -> x3, local copies, waits for them, and re-layouts: 6.52 us -> 1.67 us
where the time goes in v1:
time: 252 us; the launch traced here: 251 us
  Pallas kernels  247 us (98%)
  local copies, waits for them, and re-layouts  3.34 us (1%)
    pallas_call x1, Pallas kernels, attention_forward(): pl.pallas_call(functools.partial(forward_kernel, shards), out_shape=(jax....  92.3 us
    pallas_call x1, Pallas kernels, attention_backward(): pl.pallas_call(functools.partial(backward_kernel, shards, bits, pages), o...  66.5 us
    pallas_call x1, Pallas kernels, feed_forward(): pl.pallas_call(mlp_kernel, out_shape=(jax.ShapeDtypeStruct((rows_here, mo...  59.1 us
    pallas_call x1, Pallas kernels, reduce_grads(): pl.pallas_call(functools.partial(reduce_kernel, bits), out_shape=(jax.Sha...  24.1 us
    pallas_call x1, Pallas kernels, finish_grads(): pl.pallas_call(finish_kernel, out_shape=(jax.ShapeDtypeStruct((3, own, mo...  5.4 us

profile of v1, /device:TPU:0, one launch (start us, length us, event | category | flops | bytes accessed | tf_op | source)
XLA Modules:
  0.0 251.4 jit_solution(11697216108692262896)
XLA Ops:
  0.7 92.3 %attention_forward.1 = (bf16[4,3,768,512]{3,2,1,0:T(8,128)(2,1)}, bf16[4,12,512,512]{3,2,1,0:T(8,128)(2,1)}, f32[4,12,1,512]{3,2,1,0:T(1,128)}, bf16[4,768,512]{...) custom-call(s32[4]{0:T(128)} %counts_ref.3, ...), custom_call_target="tpu_custom_call" | custom-call | tf_op jit(solution)/shard_map/attention_forward/pallas_call | solution.py:950
  93.0 59.1 %feed_forward.1 = (bf16[2048,768]{1,0:T(8,128)(2,1)}, f32[2048,768]{1,0:T(8,128)}, bf16[768,768]{1,0:T(8,128)(2,1)}, bf16[768,768]{1,0:T(8,128)(2,1)}, f32[8,768]{1,0:T(8,128)}) custom-call(s32[4]{0:T(128)} %counts_ref.3, s32[1]{0:T(128)} %bitcast.place_ref, f32[2048,768]{1,0:T(8,128)} %get-tuple-element.45.hidden_ref, bf16[2048,768]{1,0:T(8,128)(2,1)} %cotangent_ref.1, ...), custom_call_target="tpu_custom_call" | custom-call | tf_op jit(solution)/shard_map/feed_forward/pallas_call | solution.py:1009
  152.1 66.5 %attention_backward.1 = (bf16[2048,768]{1,0:T(8,128)(2,1)}, bf16[768,768]{1,0:T(8,128)(2,1)}, f32[8,768]{1,0:T(8,128)}, bf16[768,768]{1,0:T(8,128)(2,1)}, bf16[768,768]{1,0:T(8,128)(2,1)}) custom-call(bf16[2048,768]{1,0:T(8,128)(2,1)} %x_ref.3, s32[4,1,512]{2,1,0:T(1,128)} %bitcast.19, s32[4,1,512]{2,1,0:T(1,128)} %bitcast.21, ...), custom_call_target="tpu_custom_call" | custom-call | tf_op jit(solution)/shard_map/attention_backward/pallas_call | solution.py:1075
  218.6 0.0 copy-start
  218.6 24.1 %reduce_grads.1 = (bf16[768,768]{1,0:T(8,128)(2,1)}, f32[8,768]{1,0:T(8,128)}, f32[8,768]{1,0:T(8,128)}) custom-call(bf16[768,768]{1,0:T(8,128)(2,1)} %get-tuple-element.60.part_ref, f32[8,768]{1,0:T(8,128)} %get-tuple-element.61.small_one_ref, f32[8,768]{1,0:T(8,128)} %get-tuple-element.62.small_two_ref), custom_call_target="tpu_custom_call" | custom-call | tf_op jit(solution)/shard_map/reduce_grads/pallas_call | solution.py:1142
  242.7 5.4 %finish_grads.1 = (f32[3,192,768]{2,1,0:T(8,128)}, f32[2,192]{1,0:T(2,128)}, f32[192,768]{1,0:T(8,128)}, f32[768,768]{1,0:T(8,128)}, f32[768,768]{1,0:T(8,128)}, /*index=5*/f32[3,2,64]{2,1,0:T(2,128)}, f32[8,768]{1,0:T(8,128)}) custom-call(bf16[768,768]{1,0:T(8,128)(2,1)} %get-tuple-element.63.pack_ref, bf16[768,768]{1,0:T(8,128)(2,1)} %get-tuple-element.64.up_ref, ...), custom_call_target="tpu_custom_call" | custom-call | tf_op jit(solution)/shard_map/finish_grads/pallas_call | solution.py:1161
  248.1 1.7 slice_reduce_fusion
  249.8 0.0 copy-done
  249.8 1.7 copy.35
Async XLA Ops:
  218.6 31.2 %copy-start = (bf16[2048,768]{1,0:T(8,128)(2,1)S(1)}, bf16[2048,768]{1,0:T(8,128)(2,1)}, u32[]{:S(2)}) copy-start(bf16[2048,768]{1,0:T(8,128)(2,1)} %get-tuple-element.98) | copy-start | bytes 9437188

commit v2 on v1

--- a/solution.py
+++ b/solution.py
@@ -203,13 +203,16 @@
                 later = (stage, tick)
                 start.append(later)
     start += [(3, item) for item in range(first)]
-    ready = first + 2
+    ready = min(items, first + 3)
+    start += [(0, item) for item in range(first + 2, ready)]
     groups = []
-    for tick in range(first + 1, items + 3):
-        group = [(stage, tick - stage) for stage in (3, 2, 1) if first <= tick - stage < items]
-        if ready <= tick + 1 < items:
-            group.append((0, tick + 1))
+    for tick in range(first, items + 4):
+        group = [(stage, tick - lag) for stage, lag in ((3, 4), (2, 2), (1, 0)) if first <= tick - lag < items]
+        if ready <= tick + 3 < items:
+            group.append((0, tick + 3))
         groups.append(group)
+    last = groups.pop()
+    groups[-1] = groups[-1] + last
     return start, groups
 
 
@@ -363,7 +366,7 @@
 
     def point(index):
         for at, group in enumerate(groups):
-            where = (at + 1) * points * pages // (len(groups) + 1) - 1
+            where = (at + 1) * points * pages // len(groups) - 1
             if where % points == index:
                 pl.when(page == where // points)(functools.partial(run_group, group))
 

time: 252 us -> 249 us (0.988)
    pallas_call x1, Pallas kernels: 92.3 us -> 87.9 us  [attention_forward(): pl.pallas_call(functools.partial(forward_kernel, shards), out_shape=(jax....]
where the time goes in v2:
time: 249 us
  Pallas kernels  245 us (98%)
  local copies, waits for them, and re-layouts  3.34 us (1%)
    pallas_call x1, Pallas kernels, attention_forward(): pl.pallas_call(functools.partial(forward_kernel, shards), out_shape=(jax....  87.9 us
    pallas_call x1, Pallas kernels, attention_backward(): pl.pallas_call(functools.partial(backward_kernel, shards, bits, pages), o...  67 us
    pallas_call x1, Pallas kernels, feed_forward(): pl.pallas_call(mlp_kernel, out_shape=(jax.ShapeDtypeStruct((rows_here, mo...  59.1 us
    pallas_call x1, Pallas kernels, reduce_grads(): pl.pallas_call(functools.partial(reduce_kernel, bits), out_shape=(jax.Sha...  25.8 us
    pallas_call x1, Pallas kernels, finish_grads(): pl.pallas_call(finish_kernel, out_shape=(jax.ShapeDtypeStruct((3, own, mo...  5.4 us

profile of v2, /device:TPU:0, one launch (start us, length us, event | category | flops | bytes accessed | tf_op | source)
XLA Modules:
  0.0 249.2 jit_solution(10862684461107508553)
XLA Ops:
  0.7 87.9 %attention_forward.1 = (bf16[4,3,768,512]{3,2,1,0:T(8,128)(2,1)}, bf16[4,12,512,512]{3,2,1,0:T(8,128)(2,1)}, f32[4,12,1,512]{3,2,1,0:T(1,128)}, bf16[4,768,512]{...) custom-call(s32[4]{0:T(128)} %counts_ref.3, ...), custom_call_target="tpu_custom_call" | custom-call | tf_op jit(solution)/shard_map/attention_forward/pallas_call | solution.py:953
  88.6 59.1 %feed_forward.1 = (bf16[2048,768]{1,0:T(8,128)(2,1)}, f32[2048,768]{1,0:T(8,128)}, bf16[768,768]{1,0:T(8,128)(2,1)}, bf16[768,768]{1,0:T(8,128)(2,1)}, f32[8,768]{1,0:T(8,128)}) custom-call(s32[4]{0:T(128)} %counts_ref.3, s32[1]{0:T(128)} %bitcast.place_ref, f32[2048,768]{1,0:T(8,128)} %get-tuple-element.45.hidden_ref, bf16[2048,768]{1,0:T(8,128)(2,1)} %cotangent_ref.1, ...), custom_call_target="tpu_custom_call" | custom-call | tf_op jit(solution)/shard_map/feed_forward/pallas_call | solution.py:1012
  147.7 67.0 %attention_backward.1 = (bf16[2048,768]{1,0:T(8,128)(2,1)}, bf16[768,768]{1,0:T(8,128)(2,1)}, f32[8,768]{1,0:T(8,128)}, bf16[768,768]{1,0:T(8,128)(2,1)}, bf16[768,768]{1,0:T(8,128)(2,1)}) custom-call(bf16[2048,768]{1,0:T(8,128)(2,1)} %x_ref.3, s32[4,1,512]{2,1,0:T(1,128)} %bitcast.19, s32[4,1,512]{2,1,0:T(1,128)} %bitcast.21, ...), custom_call_target="tpu_custom_call" | custom-call | tf_op jit(solution)/shard_map/attention_backward/pallas_call | solution.py:1078
  214.7 0.0 copy-start
  214.7 25.8 %reduce_grads.1 = (bf16[768,768]{1,0:T(8,128)(2,1)}, f32[8,768]{1,0:T(8,128)}, f32[8,768]{1,0:T(8,128)}) custom-call(bf16[768,768]{1,0:T(8,128)(2,1)} %get-tuple-element.60.part_ref, f32[8,768]{1,0:T(8,128)} %get-tuple-element.61.small_one_ref, f32[8,768]{1,0:T(8,128)} %get-tuple-element.62.small_two_ref), custom_call_target="tpu_custom_call" | custom-call | tf_op jit(solution)/shard_map/reduce_grads/pallas_call | solution.py:1145
  240.4 5.4 %finish_grads.1 = (f32[3,192,768]{2,1,0:T(8,128)}, f32[2,192]{1,0:T(2,128)}, f32[192,768]{1,0:T(8,128)}, f32[768,768]{1,0:T(8,128)}, f32[768,768]{1,0:T(8,128)}, /*index=5*/f32[3,2,64]{2,1,0:T(2,128)}, f32[8,768]{1,0:T(8,128)}) custom-call(bf16[768,768]{1,0:T(8,128)(2,1)} %get-tuple-element.63.pack_ref, bf16[768,768]{1,0:T(8,128)(2,1)} %get-tuple-element.64.up_ref, ...), custom_call_target="tpu_custom_call" | custom-call | tf_op jit(solution)/shard_map/finish_grads/pallas_call | solution.py:1164
  245.8 1.7 slice_reduce_fusion
  247.5 0.0 copy-done
  247.5 1.7 copy.35
Async XLA Ops:
  214.7 32.9 %copy-start = (bf16[2048,768]{1,0:T(8,128)(2,1)S(1)}, bf16[2048,768]{1,0:T(8,128)(2,1)}, u32[]{:S(2)}) copy-start(bf16[2048,768]{1,0:T(8,128)(2,1)} %get-tuple-element.98) | copy-start | bytes 9437188
